TPU v7x, 32 devices: a whole 2x2x4 slice. The times are simulated.
32 devices in a mesh: batch: 8 (over z, core), proto: 4 (over y, x).
Axes of the slice: x: 2, y: 2, z: 4, core: 2. Of those that a mesh axis runs over, the one named last changes fastest.
Arguments:
- student_features: bfloat16 [10, 1024, 256], P(None, 'batch'), may hold values from -8 to 8
- teacher_features: bfloat16 [2, 1024, 256], P(None, 'batch'), may hold values from -8 to 8
- student_prototypes: bfloat16 [256, 65536], P(None, 'proto'), may hold values from -0.5 to 0.5
- teacher_prototypes: bfloat16 [256, 65536], P(None, 'proto'), may hold values from -0.5 to 0.5
Outputs:
- mean_loss: float32 [], replicated
- grad_features: float32 [10, 1024, 256], P(None, ('batch', 'proto'))
- grad_prototypes: float32 [256, 65536], P('batch', 'proto')
All inputs are finite; a program needn't handle non-finite values.
Results may differ from a plain program's by a relative error of at most 0.001.
The roundings to bfloat16 on the way count: a program that leaves them out, or rounds other values in their place, can miss the bound.
Values sent between devices are 32-bit elements; how exact they have to be, the bound alone decides.
No kernel may reach another device: no remote copies, remote signals or barrier semaphores. Data moves between devices by JAX's collectives and lax.ppermute only.
A program may use at most 512 MiB of HBM per device.

v0:
```python
import jax
import jax.numpy as jnp
from jax import lax
from jax.sharding import PartitionSpec as P

CLUSTER_NUMBER = 65536
WIDE_CROP_NUMBER = 2
SK_ITERS = 3
PAIRS = 18
STUDENT_TEMP = 0.1
TEACHER_TEMP = 0.07
NORM_EPS = 1e-06


def unit_rows(values):
    floats = values.astype(jnp.float32)
    inverse = lax.rsqrt(jnp.sum(floats * floats, axis=-1, keepdims=True) + NORM_EPS)
    return (floats * inverse, inverse)


def unit_columns(values):
    floats = values.astype(jnp.float32)
    inverse = lax.rsqrt(jnp.sum(floats * floats, axis=0, keepdims=True) + NORM_EPS)
    return (floats * inverse, inverse)


def proto_step(cluster_share):
    column_mass = lax.psum(jnp.sum(cluster_share, axis=0), "batch")
    return cluster_share / (CLUSTER_NUMBER * column_mass[None, :])


def full_sweep(cluster_share, sample_number):
    cluster_share = proto_step(cluster_share)
    row_mass = lax.psum(jnp.sum(cluster_share, axis=1), "proto")
    return cluster_share / (sample_number * row_mass[:, None])


def on_device(student_features, teacher_features, student_prototypes, teacher_prototypes):
    crop_count, img_local, feature_dim = student_features.shape
    proto_local = student_prototypes.shape[1]
    batch_devices = lax.axis_size("batch")
    proto_devices = lax.axis_size("proto")
    images_all = img_local * batch_devices
    teacher_rows = WIDE_CROP_NUMBER * images_all
    student_count = crop_count * img_local
    unit_student, student_scale = unit_rows(student_features)
    student_bf = unit_student.astype(jnp.bfloat16).reshape(student_count, feature_dim)
    unit_proto, proto_scale = unit_columns(student_prototypes)
    proto_bf = unit_proto.astype(jnp.bfloat16)
    unit_teacher, unused_scale = unit_rows(teacher_features)
    teacher_bf = unit_teacher.astype(jnp.bfloat16).reshape(
        WIDE_CROP_NUMBER * img_local, feature_dim
    )
    unit_tproto, unused_tscale = unit_columns(teacher_prototypes)
    teacher_proto_bf = unit_tproto.astype(jnp.bfloat16)
    cluster_share = jnp.exp(
        jnp.dot(teacher_bf, teacher_proto_bf, preferred_element_type=jnp.float32) / TEACHER_TEMP
    )
    logits = jnp.dot(student_bf, proto_bf, preferred_element_type=jnp.float32) / STUDENT_TEMP
    exp_partial = jnp.sum(jnp.exp(logits), axis=1)
    for sweep_index in range(SK_ITERS):
        cluster_share = full_sweep(cluster_share, teacher_rows)
    exp_total = lax.psum(exp_partial, "proto")
    cluster_targets_matrix = (teacher_rows * cluster_share).reshape(
        WIDE_CROP_NUMBER, img_local, proto_local
    )
    first_global = cluster_targets_matrix[0]
    second_global = cluster_targets_matrix[1]
    summed = first_global + second_global
    targets = jnp.concatenate(
        [
            second_global[None],
            first_global[None],
            jnp.broadcast_to(summed[None], (crop_count - 2, img_local, proto_local)),
        ],
        axis=0,
    )
    pair_count = jnp.where(jnp.arange(crop_count) < 2, jnp.float32(1.0), jnp.float32(2.0))[
        :, None, None
    ]
    log_norm = jnp.log(exp_total).reshape(crop_count, img_local, 1)
    logits_crop = logits.reshape(crop_count, img_local, proto_local)
    loss_part = jnp.sum(targets * (log_norm - logits_crop))
    mean_loss = lax.psum(loss_part, ("batch", "proto")) / (images_all * PAIRS)
    factor = 1.0 / (images_all * PAIRS * STUDENT_TEMP)
    grad_cos = ((pair_count * jnp.exp(logits_crop - log_norm) - targets) * factor).astype(
        jnp.bfloat16
    )
    grad_cos = grad_cos.reshape(student_count, proto_local)
    feature_cot = lax.dot_general(
        grad_cos, proto_bf, (((1,), (1,)), ((), ())), preferred_element_type=jnp.float32
    )
    feature_cot = feature_cot.reshape(crop_count, img_local, feature_dim)
    own_count = img_local // proto_devices
    own_start = lax.axis_index("proto") * own_count
    cot_total = lax.psum(feature_cot, "proto")
    cot_own = lax.dynamic_slice_in_dim(cot_total, own_start, own_count, 1)
    unit_own = lax.dynamic_slice_in_dim(unit_student, own_start, own_count, 1)
    scale_own = lax.dynamic_slice_in_dim(student_scale, own_start, own_count, 1)
    grad_features = scale_own * (
        cot_own - unit_own * jnp.sum(unit_own * cot_own, axis=-1, keepdims=True)
    )
    curvature = jnp.sum(logits * STUDENT_TEMP * grad_cos.astype(jnp.float32), axis=0)
    product = lax.dot_general(
        student_bf, grad_cos, (((0,), (0,)), ((), ())), preferred_element_type=jnp.float32
    )
    term_own = lax.psum_scatter(
        product - unit_proto * curvature[None, :], "batch", scatter_dimension=0, tiled=True
    )
    grad_prototypes = proto_scale * term_own
    return (mean_loss, grad_features, grad_prototypes)


def solution(mesh):
    placed = (P(None, "batch", None), P(None, "batch", None), P(None, "proto"), P(None, "proto"))
    return jax.shard_map(
        on_device,
        mesh=mesh,
        in_specs=placed,
        out_specs=(P(), P(None, ("batch", "proto"), None), P("batch", "proto")),
        check_vma=False,
    )
```

profile of v0, /device:TPU:0, one launch (start us, length us, event | category | flops | bytes accessed | tf_op | source)
XLA Modules:
  0.0 702.0 jit_solution(659256050865896814)
XLA Ops:
  9.3 5.2 fusion.16
  14.5 13.6 %fusion.46 = (f32[16384]{0:T(1024)}, f32[256,16384]{1,0:T(8,128)}) fusion(bf16[256,256]{1,0:T(8,128)(2,1)S(1)} %bitcast.38, bf16[256,16384]{1,0:T(8,128)(2,1)} %param.7, f32[16384]{0:T(1024)S(1)} %add_rsqrt_fusion.1), kind=kOutput, calls=%fused_computation.80 | convolution fusion | flops 2168438784 | bytes 25427968 | tf_op jit(solution)/shard_map/dot_general | solution.py:57
  30.3 5.3 fusion.18
  35.7 57.4 %broadcast_multiply_fusion = (f32[1280,16384]{1,0:T(8,128)}, f32[1280]{0:T(1024)S(1)}, f32[1280,16384]{1,0:T(8,128)}) fusion(bf16[1280,256]{1,0:T(8,128)(2,1)S(1)} %bitcast.37, bf16[256,16384]{1,0:T(8,128)(2,1)} %param.6, f32[16384]{0:T(1024)S(1)} %add_rsqrt_fusion), kind=kOutput, calls=%fused_computation.10 | convolution fusion | flops 10791943168 | bytes 176886784 | tf_op jit(solution)/shard_map/dot_general | solution.py:59
  94.0 7.2 %divide_reduce_fusion = f32[256]{0:T(256)S(1)} fusion(f32[256,16384]{1,0:T(8,128)} %get-tuple-element.18, f32[16384]{0:T(1024)S(1)} %broadcast_multiply_fusion.4), kind=kLoop, calls=%fused_computation.35 | loop fusion | flops 8388352 | bytes 16843776 | tf_op jit(solution)/shard_map/reduce_sum | solution.py:34
  101.2 11.5 %psum.64 = f32[256]{0:T(256)S(1)} all-reduce(f32[256]{0:T(256)S(1)} %divide_reduce_fusion), channel_id=1, replica_groups=mesh['batch'=8,'proto'=4] {'proto'}, use_global_device_ids=true, to_apply=%region_5.0 | all-reduce | flops 256 | bytes 2048 | tf_op jit(solution)/shard_map/psum | solution.py:34
  112.7 9.1 %fusion.21 = f32[16384]{0:T(1024)} fusion(f32[256,16384]{1,0:T(8,128)} %get-tuple-element.18, f32[256]{0:T(256)S(1)} %broadcast_multiply_fusion.7, f32[16384]{0:T(1024)S(1)} %broadcast_multiply_fusion.4), kind=kLoop, calls=%fused_computation.36 | loop fusion | flops 12566528 | bytes 16909312 | tf_op jit(solution)/shard_map/reduce_sum | solution.py:28
  121.9 54.2 %all-reduce.8.cloned.1.call-done = f32[16384]{0:T(1024)} async-done(((f32[16384]{0:T(1024)}), f32[16384]{0:T(1024)}) %all-reduce.8.cloned.1.call-update) | async-done | bytes 65552 | tf_op jit(solution)/shard_map/psum | solution.py:28
  176.9 8.6 %fusion.22 = f32[256]{0:T(256)S(1)} fusion(f32[256,16384]{1,0:T(8,128)} %get-tuple-element.18, f32[16384]{0:T(1024)S(1)} %broadcast_multiply_fusion.3, f32[256]{0:T(256)S(1)} %broadcast_multiply_fusion.7, f32[16384]{0:T(1024)S(1)} %broadcast_multiply_fusion.4), kind=kLoop, calls=%fused_computation.37 | loop fusion | flops 16776960 | bytes 16910336 | tf_op jit(solution)/shard_map/reduce_sum | solution.py:34
  185.6 9.8 %psum.66 = f32[256]{0:T(256)S(1)} all-reduce(f32[256]{0:T(256)S(1)} %fusion.22), channel_id=1, replica_groups=mesh['batch'=8,'proto'=4] {'proto'}, use_global_device_ids=true, to_apply=%region_9.0 | all-reduce | flops 256 | bytes 2048 | tf_op jit(solution)/shard_map/psum | solution.py:34
  195.4 8.8 %fusion.23 = f32[16384]{0:T(1024)} fusion(f32[256,16384]{1,0:T(8,128)} %get-tuple-element.18, f32[256]{0:T(256)S(1)} %broadcast_multiply_fusion.6, f32[16384]{0:T(1024)S(1)} %broadcast_multiply_fusion.3, f32[256]{0:T(256)S(1)} %broadcast_multiply_fusion.7, f32[16384]{0:T(1024)S(1)} %broadcast_multiply_fusion.4), kind=kLoop, calls=%fused_computation.38 | loop fusion | flops 20955136 | bytes 16975872 | tf_op jit(solution)/shard_map/reduce_sum | solution.py:28
  204.3 52.0 %all-reduce.10.cloned.1.call-done = f32[16384]{0:T(1024)} async-done(((f32[16384]{0:T(1024)}), f32[16384]{0:T(1024)}) %all-reduce.10.cloned.1.call-update) | async-done | bytes 65552 | tf_op jit(solution)/shard_map/psum | solution.py:28
  257.2 8.1 %fusion.24 = f32[256]{0:T(256)S(1)} fusion(f32[256,16384]{1,0:T(8,128)} %get-tuple-element.18, f32[16384]{0:T(1024)S(1)} %broadcast_multiply_fusion.2, f32[256]{0:T(256)S(1)} %broadcast_multiply_fusion.6, f32[16384]{0:T(1024)S(1)} %broadcast_multiply_fusion.3, f32[256]{0:T(256)S(1)} %broadcast_multiply_fusion.7, f32[16384]{0:T(1024)S(1)} %broadcast_multiply_fusion.4), kind=kLoop, calls=%fused_computation.39 | loop fusion | flops 25165568 | bytes 16976896 | tf_op jit(solution)/shard_map/reduce_sum | solution.py:34
  265.3 10.4 %all-reduce = (f32[256]{0:T(256)S(1)}, f32[1280]{0:T(1024)S(1)}) all-reduce(f32[256]{0:T(256)S(1)} %fusion.24, f32[1280]{0:T(1024)S(1)} %get-tuple-element.9), channel_id=1, replica_groups=mesh['batch'=8,'proto'=4] {'proto'}, use_global_device_ids=true, to_apply=%region_13.0 | all-reduce | flops 1536 | bytes 12288 | tf_op jit(solution)/shard_map/psum | solution.py:34
  275.7 12.9 %fusion.20 = f32[256,16384]{1,0:T(8,128)} fusion(f32[256,16384]{1,0:T(8,128)} %get-tuple-element.18, f32[256]{0:T(256)S(1)} %broadcast_multiply_fusion.5, f32[16384]{0:T(1024)S(1)} %broadcast_multiply_fusion.2, f32[256]{0:T(256)S(1)} %broadcast_multiply_fusion.6, f32[16384]{0:T(1024)S(1)} %broadcast_multiply_fusion.3, f32[256]{0:T(256)S(1)} %broadcast_multiply_fusion.7, ...), kind=kLoop, calls=%fused_computation.34 | loop fusion | flops 29360128 | bytes 33754112 | tf_op jit(solution)/shard_map/mul | solution.py:64
  288.6 10.6 %slice_bitcast_fusion.1 = (f32[1,128,16384]{2,1,0:T(8,128)}, f32[128,16384]{1,0:T(8,128)S(1)}, f32[1,128,16384]{2,1,0:T(8,128)}) fusion(f32[256,16384]{1,0:T(8,128)} %fusion.20), kind=kLoop, calls=%fused_computation.45 | loop fusion | flops 2097152 | bytes 41943040 | tf_op jit(solution)/shard_map/slice | solution.py:68
  299.2 21.2 %broadcast_in_dim.8 = f32[8,128,16384]{2,1,0:T(8,128)} broadcast(f32[128,16384]{1,0:T(8,128)S(1)} %get-tuple-element.11), dimensions={1,2} | broadcast | bytes 75497472 | tf_op jit(solution)/shard_map/broadcast_in_dim | solution.py:74
  320.3 53.8 %pad_maximum_fusion = f32[10,128,16384]{2,1,0:T(8,128)} fusion(f32[8,128,16384]{2,1,0:T(8,128)} %broadcast_in_dim.8, f32[1,128,16384]{2,1,0:T(8,128)} %get-tuple-element.12, f32[1,128,16384]{2,1,0:T(8,128)} %get-tuple-element.10), kind=kLoop, calls=%fused_computation.1 | loop fusion | flops 41943040 | bytes 167772160 | tf_op jit(solution)/shard_map/concatenate | solution.py:70
  374.2 66.4 %multiply_reduce_fusion = (f32[16384]{0:T(1024)S(1)}, f32[]{:T(128)}, bf16[1280,16384]{1,0:T(8,128)(2,1)}) fusion(f32[1280,16384]{1,0:T(8,128)} %get-tuple-element.19, f32[1280]{0:T(1024)S(1)} %get-tuple-element.16, f32[10,128,16384]{2,1,0:T(8,128)} %pad_maximum_fusion, f32[1280]{0:T(1024)S(1)} %broadcast_bitcast_fusion), kind=kLoop, calls=%fused_computation.7 | loop fusion | flops 251641856 | bytes 209790976 | tf_op jit(solution)/shard_map/reduce_sum | solution.py:103
  440.5 20.8 %fusion.26 = f32[10,128,256]{2,1,0:T(8,128)} fusion(bf16[10,128,16384]{2,1,0:T(8,128)(2,1)} %bitcast.36, bf16[256,16384]{1,0:T(8,128)(2,1)} %param.6, f32[16384]{0:T(1024)S(1)} %copy-done.5), kind=kOutput, calls=%fused_computation.40 | convolution fusion | flops 10750001152 | bytes 51707904 | tf_op jit(solution)/shard_map/dot_general | solution.py:90
  461.4 62.9 %fusion.11 = f32[256,16384]{1,0:T(8,128)} fusion(bf16[10,128,256]{2,1,0:T(8,128)(2,1)S(1)} %copy-done.3, f32[10,128,16384]{2,1,0:T(8,128)} %bitcast.8, f32[10,128]{1,0:T(8,128)S(1)} %get-tuple-element.15, f32[10]{0:T(128)S(1)} %copy-done.9, bf16[256,16384]{1,0:T(8,128)(2,1)} %param.6, f32[8,128,16384]{2,1,0:T(8,128)} %broadcast_in_dim.8, ...), kind=kOutput, calls=%fused_computation.21 | convolution fusion | flops 10900996096 | bytes 193729568 | tf_op jit(solution)/shard_map/dot_general | solution.py:104
  525.1 40.3 %psum.70 = f32[]{:T(128)} all-reduce(f32[]{:T(128)} %get-tuple-element.4), channel_id=1, replica_groups=mesh['batch'=8,'proto'=4] {'batch','proto'}, use_global_device_ids=true, to_apply=%region_19.20 | all-reduce | flops 1 | bytes 8 | tf_op jit(solution)/shard_map/psum | solution.py:84
  568.5 122.7 %reduce-scatter.2.cloned.1.call-done = f32[32,16384]{1,0:T(8,128)} async-done(((f32[256,16384]{1,0:T(8,128)}), f32[32,16384]{1,0:T(8,128)}) %reduce-scatter.2.cloned.1.call-update) | async-done | bytes 2097168 | tf_op jit(solution)/shard_map/reduce_scatter | solution.py:107
  691.2 3.1 broadcast_multiply_fusion.1
  (51 shorter events, 10.3 us)
Async XLA Ops:
  7.2 86.0 %all-reduce.6.cloned.1.call-start = ((), (), s32[]{:S(2)}) async-start(), calls=%async_computation.1 | async-start | bytes 131072 | tf_op jit(solution)/shard_map/psum | solution.py:28
  9.3 18.9 %copy-start.1 = (bf16[10,128,256]{2,1,0:T(8,128)(2,1)S(1)}, bf16[10,128,256]{2,1,0:T(8,128)(2,1)}, u32[]{:S(2)}) copy-start(bf16[10,128,256]{2,1,0:T(8,128)(2,1)} %param.4) | copy-start | bytes 1966084
  28.1 148.0 %all-reduce.8.cloned.1.call-start = ((), (), s32[]{:S(2)}) async-start(), calls=%async_computation.2 | async-start | bytes 131072 | tf_op jit(solution)/shard_map/psum | solution.py:28
  28.4 0.6 copy-start.6
  30.3 62.8 %copy-start.2 = (bf16[10,128,256]{2,1,0:T(8,128)(2,1)}, bf16[10,128,256]{2,1,0:T(8,128)(2,1)S(1)}, u32[]{:S(2)}) copy-start(bf16[10,128,256]{2,1,0:T(8,128)(2,1)S(1)} %get-tuple-element.14) | copy-start | bytes 1966084
  35.7 57.4 %copy-start.4 = (f32[16384]{0:T(1024)}, f32[16384]{0:T(1024)S(1)}, u32[]{:S(2)}) copy-start(f32[16384]{0:T(1024)S(1)} %add_rsqrt_fusion) | copy-start | bytes 196612
  121.8 134.6 %all-reduce.10.cloned.1.call-start = ((), (), s32[]{:S(2)}) async-start(), calls=%async_computation.3 | async-start | bytes 131072 | tf_op jit(solution)/shard_map/psum | solution.py:28
  121.9 82.4 %copy-start.8 = (f32[10]{0:T(128)}, f32[10]{0:T(128)S(1)}, u32[]{:S(2)}) copy-start(f32[10]{0:T(128)S(1)} %compare_select_fusion) | copy-start | bytes 124
  204.2 361.9 %all-reduce.12.cloned.1.call-start = ((), (), s32[]{:S(2)}) async-start(), calls=%async_computation.4 | async-start | bytes 2621440 | tf_op jit(solution)/shard_map/psum | solution.py:96
  374.1 66.4 %copy-start.5 = (f32[16384]{0:T(1024)S(1)}, f32[16384]{0:T(1024)}, u32[]{:S(2)}) copy-start(f32[16384]{0:T(1024)} %copy-done.4) | copy-start | bytes 196612
  440.5 20.9 %copy-start.3 = (bf16[10,128,256]{2,1,0:T(8,128)(2,1)S(1)}, bf16[10,128,256]{2,1,0:T(8,128)(2,1)}, u32[]{:S(2)}) copy-start(bf16[10,128,256]{2,1,0:T(8,128)(2,1)} %copy-done.2) | copy-start | bytes 1966084
  440.5 20.9 %copy-start.9 = (f32[10]{0:T(128)S(1)}, f32[10]{0:T(128)}, u32[]{:S(2)}) copy-start(f32[10]{0:T(128)} %copy-done.8) | copy-start | bytes 124
  461.3 229.9 %reduce-scatter.2.cloned.1.call-start = ((), (), s32[]{:S(2)}) async-start(), calls=%async_computation.5 | async-start | bytes 18874368 | tf_op jit(solution)/shard_map/reduce_scatter | solution.py:107
  524.3 0.7 copy-start.7
  524.3 41.8 %copy-start = (f32[10,128,256]{2,1,0:T(8,128)S(1)}, f32[10,128,256]{2,1,0:T(8,128)}, u32[]{:S(2)}) copy-start(f32[10,128,256]{2,1,0:T(8,128)} %get-tuple-element.13) | copy-start | bytes 3932164
Sparse Core Ops, SparseCore 0:
  28.2 57.4 all-reduce.5
  121.9 54.1 all-reduce.7
  204.3 51.9 all-reduce.9
  461.4 53.5 all-reduce.11
  524.5 166.7 reduce-scatter.1
where the time goes:
time: 703 us; the launch traced here: 702 us
  waiting for transfers between devices  229 us (33%)
  other arithmetic  208 us (30%)
  matrix products  155 us (22%)
  blocking collectives  72.1 us (10%)
  local copies, waits for them, and re-layouts  22.6 us (3%)
  between operations  15.8 us (2%)
    reduce_scatter x1, waiting for transfers between devices, on_device(): lax.psum_scatter(product - unit_proto * curvature[None, :], 'batch', scat...  123 us
    psum x3, waiting for transfers between devices, proto_step(): column_mass = lax.psum(jnp.sum(cluster_share, axis=0), 'batch')  106 us
    reduce_sum x1, other arithmetic, on_device(): jnp.sum(logits * STUDENT_TEMP * grad_cos.astype(jnp.float32), axis=0)  66.4 us
    dot_general x1, matrix products, on_device(): lax.dot_general(student_bf, grad_cos, (((0,), (0,)), ((), ())), preferred...  62.9 us
    dot_general x1, matrix products, on_device(): jnp.dot(student_bf, proto_bf, preferred_element_type=jnp.float32)  57.4 us
    concatenate x1, other arithmetic, on_device(): jnp.concatenate([second_global[None], first_global[None], jnp.broadcast_t...  53.8 us
    psum x1, blocking collectives, on_device(): mean_loss = lax.psum(loss_part, ('batch', 'proto')) / (images_all * PAIRS)  40.3 us
    psum x3, blocking collectives, full_sweep(): row_mass = lax.psum(jnp.sum(cluster_share, axis=1), 'proto')  31.8 us
  transfers between devices with their start and end apart: 5, of which 3 were waited for; matrix products, arithmetic and copies ran while one was open for 18% of the time, Pallas kernels for 0%

commit v1 on v0

--- a/solution.py
+++ b/solution.py
@@ -25,7 +25,7 @@
 
 
 def proto_step(cluster_share):
-    column_mass = lax.psum(jnp.sum(cluster_share, axis=0), "batch")
+    column_mass = jnp.sum(lax.all_gather(jnp.sum(cluster_share, axis=0), "batch"), axis=0)
     return cluster_share / (CLUSTER_NUMBER * column_mass[None, :])
 
 

time: 703 us -> 638 us (0.908)
  waiting for transfers between devices: 229 us -> 125 us
  blocking collectives: 72.1 us -> 115 us
    psum x3 -> x0, waiting for transfers between devices: 106 us -> none  [proto_step(): column_mass = lax.psum(jnp.sum(cluster_share, axis=0), 'batch')]
    all_gather x0 -> x3, blocking collectives: none -> 46.6 us  [proto_step(): lax.all_gather(jnp.sum(cluster_share, axis=0), 'batch')]
    reduce_sum x2 -> x5, other arithmetic: 17.8 us -> 17 us  [the longest x2 16.6 us: proto_step(): jnp.sum(cluster_share, axis=0)]
  transfers between devices with their start and end apart: 5 -> 2, of which waited for: 3 -> 1; matrix products, arithmetic and copies ran while one was open for 18% -> 10% of each run, Pallas kernels for 0% -> 0%
where the time goes in v1:
time: 638 us
  other arithmetic  204 us (32%)
  matrix products  154 us (24%)
  waiting for transfers between devices  125 us (20%)
  blocking collectives  115 us (18%)
  local copies, waits for them, and re-layouts  21.6 us (3%)
  between operations  17.5 us (3%)
    reduce_scatter x1, waiting for transfers between devices, on_device(): lax.psum_scatter(product - unit_proto * curvature[None, :], 'batch', scat...  125 us
    reduce_sum x1, other arithmetic, on_device(): jnp.sum(logits * STUDENT_TEMP * grad_cos.astype(jnp.float32), axis=0)  66.3 us
    dot_general x1, matrix products, on_device(): lax.dot_general(student_bf, grad_cos, (((0,), (0,)), ((), ())), preferred...  63.3 us
    dot_general x1, matrix products, on_device(): jnp.dot(student_bf, proto_bf, preferred_element_type=jnp.float32)  57.3 us
    concatenate x1, other arithmetic, on_device(): jnp.concatenate([second_global[None], first_global[None], jnp.broadcast_t...  53.8 us
    all_gather x3, blocking collectives, proto_step(): lax.all_gather(jnp.sum(cluster_share, axis=0), 'batch')  46.6 us
    psum x1, blocking collectives, on_device(): mean_loss = lax.psum(loss_part, ('batch', 'proto')) / (images_all * PAIRS)  41 us
    psum x3, blocking collectives, full_sweep(): row_mass = lax.psum(jnp.sum(cluster_share, axis=1), 'proto')  27.4 us
  transfers between devices with their start and end apart: 2, of which 1 were waited for; matrix products, arithmetic and copies ran while one was open for 10% of the time, Pallas kernels for 0%

profile of v1, /device:TPU:0, one launch (start us, length us, event | category | flops | bytes accessed | tf_op | source)
XLA Modules:
  0.0 637.6 jit_solution(7024652313688676178)
XLA Ops:
  10.1 5.1 fusion.16
  15.2 13.0 %fusion.46 = (f32[16384]{0:T(1024)S(1)}, f32[256,16384]{1,0:T(8,128)}) fusion(bf16[256,256]{1,0:T(8,128)(2,1)S(1)} %bitcast.38, bf16[256,16384]{1,0:T(8,128)(2,1)} %param.7, f32[16384]{0:T(1024)S(1)} %add_rsqrt_fusion.1), kind=kOutput, calls=%fused_computation.80 | convolution fusion | flops 2168438784 | bytes 25427968 | tf_op jit(solution)/shard_map/dot_general | solution.py:57
  28.2 16.5 %all-gather = f32[131072]{0:T(1024)S(1)} all-gather(f32[16384]{0:T(1024)S(1)} %get-tuple-element.17), channel_id=2, replica_groups=mesh['batch'=8,'proto'=4] {'batch'}, dimensions={0}, use_global_device_ids=true | all-gather | bytes 589824 | tf_op jit(solution)/shard_map/all_gather | solution.py:28
  45.0 7.2 %divide_reduce_fusion = f32[256]{0:T(256)S(1)} fusion(f32[256,16384]{1,0:T(8,128)} %get-tuple-element.18, f32[16384]{0:T(1024)S(1)} %broadcast_multiply_fusion.4), kind=kLoop, calls=%fused_computation.35 | loop fusion | flops 8388352 | bytes 16843776 | tf_op jit(solution)/shard_map/reduce_sum | solution.py:34
  52.2 9.9 %psum.42 = f32[256]{0:T(256)S(1)} all-reduce(f32[256]{0:T(256)S(1)} %divide_reduce_fusion), channel_id=1, replica_groups=mesh['batch'=8,'proto'=4] {'proto'}, use_global_device_ids=true, to_apply=%region_5.0 | all-reduce | flops 256 | bytes 2048 | tf_op jit(solution)/shard_map/psum | solution.py:34
  62.1 8.4 %fusion.21 = f32[16384]{0:T(1024)S(1)} fusion(f32[256,16384]{1,0:T(8,128)} %get-tuple-element.18, f32[256]{0:T(256)S(1)} %broadcast_multiply_fusion.7, f32[16384]{0:T(1024)S(1)} %broadcast_multiply_fusion.4), kind=kLoop, calls=%fused_computation.36 | loop fusion | flops 12566528 | bytes 16909312 | tf_op jit(solution)/shard_map/reduce_sum | solution.py:28
  70.5 15.2 %all-gather.1 = f32[131072]{0:T(1024)S(1)} all-gather(f32[16384]{0:T(1024)S(1)} %fusion.21), channel_id=3, replica_groups=mesh['batch'=8,'proto'=4] {'batch'}, dimensions={0}, use_global_device_ids=true | all-gather | bytes 589824 | tf_op jit(solution)/shard_map/all_gather | solution.py:28
  85.9 8.7 %fusion.22 = f32[256]{0:T(256)S(1)} fusion(f32[256,16384]{1,0:T(8,128)} %get-tuple-element.18, f32[16384]{0:T(1024)S(1)} %broadcast_multiply_fusion.3, f32[256]{0:T(256)S(1)} %broadcast_multiply_fusion.7, f32[16384]{0:T(1024)S(1)} %broadcast_multiply_fusion.4), kind=kLoop, calls=%fused_computation.37 | loop fusion | flops 16776960 | bytes 16910336 | tf_op jit(solution)/shard_map/reduce_sum | solution.py:34
  94.6 8.0 %psum.43 = f32[256]{0:T(256)S(1)} all-reduce(f32[256]{0:T(256)S(1)} %fusion.22), channel_id=1, replica_groups=mesh['batch'=8,'proto'=4] {'proto'}, use_global_device_ids=true, to_apply=%region_9.0 | all-reduce | flops 256 | bytes 2048 | tf_op jit(solution)/shard_map/psum | solution.py:34
  102.5 8.2 %fusion.23 = f32[16384]{0:T(1024)S(1)} fusion(f32[256,16384]{1,0:T(8,128)} %get-tuple-element.18, f32[256]{0:T(256)S(1)} %broadcast_multiply_fusion.6, f32[16384]{0:T(1024)S(1)} %broadcast_multiply_fusion.3, f32[256]{0:T(256)S(1)} %broadcast_multiply_fusion.7, f32[16384]{0:T(1024)S(1)} %broadcast_multiply_fusion.4), kind=kLoop, calls=%fused_computation.38 | loop fusion | flops 20955136 | bytes 16975872 | tf_op jit(solution)/shard_map/reduce_sum | solution.py:28
  110.8 14.9 %all-gather.2 = f32[131072]{0:T(1024)S(1)} all-gather(f32[16384]{0:T(1024)S(1)} %fusion.23), channel_id=4, replica_groups=mesh['batch'=8,'proto'=4] {'batch'}, dimensions={0}, use_global_device_ids=true | all-gather | bytes 589824 | tf_op jit(solution)/shard_map/all_gather | solution.py:28
  125.9 8.1 %fusion.24 = f32[256]{0:T(256)S(1)} fusion(f32[256,16384]{1,0:T(8,128)} %get-tuple-element.18, f32[16384]{0:T(1024)S(1)} %broadcast_multiply_fusion.2, f32[256]{0:T(256)S(1)} %broadcast_multiply_fusion.6, f32[16384]{0:T(1024)S(1)} %broadcast_multiply_fusion.3, f32[256]{0:T(256)S(1)} %broadcast_multiply_fusion.7, f32[16384]{0:T(1024)S(1)} %broadcast_multiply_fusion.4), kind=kLoop, calls=%fused_computation.39 | loop fusion | flops 25165568 | bytes 16976896 | tf_op jit(solution)/shard_map/reduce_sum | solution.py:34
  135.6 5.3 fusion.18
  141.0 57.3 %broadcast_multiply_fusion = (f32[1280,16384]{1,0:T(8,128)}, f32[1280]{0:T(1024)S(1)}, f32[1280,16384]{1,0:T(8,128)}) fusion(bf16[1280,256]{1,0:T(8,128)(2,1)S(1)} %bitcast.37, bf16[256,16384]{1,0:T(8,128)(2,1)} %param.6, f32[16384]{0:T(1024)S(1)} %add_rsqrt_fusion), kind=kOutput, calls=%fused_computation.10 | convolution fusion | flops 10791943168 | bytes 176886784 | tf_op jit(solution)/shard_map/dot_general | solution.py:59
  198.2 9.5 %all-reduce = (f32[256]{0:T(256)S(1)}, f32[1280]{0:T(1024)S(1)}) all-reduce(f32[256]{0:T(256)S(1)} %fusion.24, f32[1280]{0:T(1024)S(1)} %get-tuple-element.9), channel_id=1, replica_groups=mesh['batch'=8,'proto'=4] {'proto'}, use_global_device_ids=true, to_apply=%region_13.0 | all-reduce | flops 1536 | bytes 12288 | tf_op jit(solution)/shard_map/psum | solution.py:34
  207.8 12.9 %fusion.20 = f32[256,16384]{1,0:T(8,128)} fusion(f32[256,16384]{1,0:T(8,128)} %get-tuple-element.18, f32[256]{0:T(256)S(1)} %broadcast_multiply_fusion.5, f32[16384]{0:T(1024)S(1)} %broadcast_multiply_fusion.2, f32[256]{0:T(256)S(1)} %broadcast_multiply_fusion.6, f32[16384]{0:T(1024)S(1)} %broadcast_multiply_fusion.3, f32[256]{0:T(256)S(1)} %broadcast_multiply_fusion.7, ...), kind=kLoop, calls=%fused_computation.34 | loop fusion | flops 29360128 | bytes 33754112 | tf_op jit(solution)/shard_map/mul | solution.py:64
  220.7 10.6 %slice_bitcast_fusion.1 = (f32[1,128,16384]{2,1,0:T(8,128)}, f32[128,16384]{1,0:T(8,128)S(1)}, f32[1,128,16384]{2,1,0:T(8,128)}) fusion(f32[256,16384]{1,0:T(8,128)} %fusion.20), kind=kLoop, calls=%fused_computation.45 | loop fusion | flops 2097152 | bytes 41943040 | tf_op jit(solution)/shard_map/slice | solution.py:68
  231.3 21.1 %broadcast_in_dim.8 = f32[8,128,16384]{2,1,0:T(8,128)} broadcast(f32[128,16384]{1,0:T(8,128)S(1)} %get-tuple-element.11), dimensions={1,2} | broadcast | bytes 75497472 | tf_op jit(solution)/shard_map/broadcast_in_dim | solution.py:74
  252.4 53.8 %pad_maximum_fusion = f32[10,128,16384]{2,1,0:T(8,128)} fusion(f32[8,128,16384]{2,1,0:T(8,128)} %broadcast_in_dim.8, f32[1,128,16384]{2,1,0:T(8,128)} %get-tuple-element.12, f32[1,128,16384]{2,1,0:T(8,128)} %get-tuple-element.10), kind=kLoop, calls=%fused_computation.1 | loop fusion | flops 41943040 | bytes 167772160 | tf_op jit(solution)/shard_map/concatenate | solution.py:70
  306.2 66.3 %multiply_reduce_fusion = (f32[16384]{0:T(1024)S(1)}, f32[]{:T(128)}, bf16[1280,16384]{1,0:T(8,128)(2,1)}) fusion(f32[1280,16384]{1,0:T(8,128)} %get-tuple-element.19, f32[1280]{0:T(1024)S(1)} %get-tuple-element.16, f32[10,128,16384]{2,1,0:T(8,128)} %pad_maximum_fusion, f32[1280]{0:T(1024)S(1)} %broadcast_bitcast_fusion), kind=kLoop, calls=%fused_computation.7 | loop fusion | flops 251641856 | bytes 209790976 | tf_op jit(solution)/shard_map/reduce_sum | solution.py:103
  372.6 20.8 %fusion.26 = f32[10,128,256]{2,1,0:T(8,128)} fusion(bf16[10,128,16384]{2,1,0:T(8,128)(2,1)} %bitcast.36, bf16[256,16384]{1,0:T(8,128)(2,1)} %param.6, f32[16384]{0:T(1024)S(1)} %add_rsqrt_fusion), kind=kOutput, calls=%fused_computation.40 | convolution fusion | flops 10750001152 | bytes 51707904 | tf_op jit(solution)/shard_map/dot_general | solution.py:90
  393.4 63.3 %fusion.11 = f32[256,16384]{1,0:T(8,128)} fusion(bf16[10,128,256]{2,1,0:T(8,128)(2,1)S(1)} %copy-done.3, f32[10,128,16384]{2,1,0:T(8,128)} %bitcast.8, f32[10,128]{1,0:T(8,128)S(1)} %get-tuple-element.15, f32[10]{0:T(128)S(1)} %compare_select_fusion, bf16[256,16384]{1,0:T(8,128)(2,1)} %param.6, f32[8,128,16384]{2,1,0:T(8,128)} %broadcast_in_dim.8, ...), kind=kOutput, calls=%fused_computation.21 | convolution fusion | flops 10900996096 | bytes 193729568 | tf_op jit(solution)/shard_map/dot_general | solution.py:104
  456.7 41.0 %psum.46 = f32[]{:T(128)} all-reduce(f32[]{:T(128)} %get-tuple-element.4), channel_id=1, replica_groups=mesh['batch'=8,'proto'=4] {'batch','proto'}, use_global_device_ids=true, to_apply=%region_19.20 | all-reduce | flops 1 | bytes 8 | tf_op jit(solution)/shard_map/psum | solution.py:84
  500.9 125.1 %reduce-scatter.2.cloned.1.call-done = f32[32,16384]{1,0:T(8,128)} async-done(((f32[256,16384]{1,0:T(8,128)}), f32[32,16384]{1,0:T(8,128)}) %reduce-scatter.2.cloned.1.call-update) | async-done | bytes 2097168 | tf_op jit(solution)/shard_map/reduce_scatter | solution.py:107
  (43 shorter events, 10.1 us)
Async XLA Ops:
  8.0 490.5 %all-reduce.3.cloned.1.call-start = ((), (), s32[]{:S(2)}) async-start(), calls=%async_computation.1 | async-start | bytes 2621440 | tf_op jit(solution)/shard_map/psum | solution.py:96
  102.5 31.5 %copy-start.1 = (bf16[10,128,256]{2,1,0:T(8,128)(2,1)S(1)}, bf16[10,128,256]{2,1,0:T(8,128)(2,1)}, u32[]{:S(2)}) copy-start(bf16[10,128,256]{2,1,0:T(8,128)(2,1)} %param.4) | copy-start | bytes 1966084
  134.3 1.3 copy-start.4
  135.6 62.7 %copy-start.2 = (bf16[10,128,256]{2,1,0:T(8,128)(2,1)}, bf16[10,128,256]{2,1,0:T(8,128)(2,1)S(1)}, u32[]{:S(2)}) copy-start(bf16[10,128,256]{2,1,0:T(8,128)(2,1)S(1)} %get-tuple-element.14) | copy-start | bytes 1966084
  372.6 20.9 %copy-start.3 = (bf16[10,128,256]{2,1,0:T(8,128)(2,1)S(1)}, bf16[10,128,256]{2,1,0:T(8,128)(2,1)}, u32[]{:S(2)}) copy-start(bf16[10,128,256]{2,1,0:T(8,128)(2,1)} %copy-done.2) | copy-start | bytes 1966084
  393.4 232.6 %reduce-scatter.2.cloned.1.call-start = ((), (), s32[]{:S(2)}) async-start(), calls=%async_computation.2 | async-start | bytes 18874368 | tf_op jit(solution)/shard_map/reduce_scatter | solution.py:107
  456.7 41.7 %copy-start.5 = (f32[10,128]{1,0:T(8,128)S(1)}, f32[10,128]{1,0:T(8,128)}, u32[]{:S(2)}) copy-start(f32[10,128]{1,0:T(8,128)} %copy-done.4) | copy-start | bytes 15364
  456.7 41.8 %copy-start = (f32[10,128,256]{2,1,0:T(8,128)S(1)}, f32[10,128,256]{2,1,0:T(8,128)}, u32[]{:S(2)}) copy-start(f32[10,128,256]{2,1,0:T(8,128)} %get-tuple-element.13) | copy-start | bytes 3932164
Sparse Core Ops, SparseCore 0:
  393.5 56.3 all-reduce.2
Sparse Core Ops, SparseCore 1:
  456.8 169.1 reduce-scatter.1
